TPU v7x, 512 devices: a whole 4x4x16 slice. The times are simulated.
512 devices in a mesh: grid: 32 (over x, y, core), band: 16 (over z).
Axes of the slice: x: 4, y: 4, z: 16, core: 2. Of those that a mesh axis runs over, the one named last changes fastest.
Arguments:
- orbitals: bfloat16 [32768, 512], P('grid', 'band'), may hold values from -6 to 6
- rotation: bfloat16 [512, 32768], P('grid', 'band'), may hold values from -0.25 to 0.25
Outputs:
- rotated: bfloat16 [32768, 32768], P('grid', 'band')
All inputs are finite; a program needn't handle non-finite values.
Results may differ from a plain program's by a relative error of at most 0.001.
Values may be sent and summed in bfloat16 or wider, within the bound.
No kernel may reach another device: no remote copies, remote signals or barrier semaphores. Data moves between devices by JAX's collectives and lax.ppermute only.
A program may use at most 64 MiB of HBM per device.

v0:
```python
import jax
import jax.numpy as jnp
from jax import lax
from jax.sharding import PartitionSpec as P


def on_device(orbitals, rotation):
    all_cols = lax.all_gather(orbitals, "band", axis=1, tiled=True)
    all_rows = lax.all_gather(rotation, "grid", axis=0, tiled=True)
    total = jnp.dot(all_cols, all_rows, preferred_element_type=jnp.float32)
    return total.astype(jnp.bfloat16)


def solution(mesh):
    in_specs = (P("grid", "band"), P("grid", "band"))
    out_specs = P("grid", "band")
    return jax.shard_map(
        on_device, mesh=mesh, in_specs=in_specs, out_specs=out_specs, check_vma=False
    )
```

profile of v0, /device:TPU:1, one launch (start us, length us, event | category | flops | bytes accessed | tf_op | source)
XLA Modules:
  0.0 158.6 jit_solution(7569212816232975436)
XLA Ops:
  6.5 0.0 all-gather.3.cloned.1.call-start
  6.5 0.7 all-gather.3.cloned.1.call-update
  7.3 0.0 all-gather.5.cloned.1.call-start
  7.3 0.7 all-gather.5.cloned.1.call-update
  8.0 68.3 %all-gather.3.cloned.1.call-done = bf16[1024,512]{0,1:T(8,128)(2,1)} async-done(((bf16[1024,32]{0,1:T(8,128)(2,1)}), bf16[1024,512]{0,1:T(8,128)(2,1)}) %all-gather.3.cloned.1.call-update) | async-done | bytes 1048592 | tf_op jit(solution)/shard_map/all_gather | solution.py:8
  76.3 69.1 %all-gather.5.cloned.1.call-done = bf16[512,2048]{1,0:T(8,128)(2,1)} async-done(((bf16[16,2048]{1,0:T(8,128)(2,1)}), bf16[512,2048]{1,0:T(8,128)(2,1)}) %all-gather.5.cloned.1.call-update) | async-done | bytes 2097168 | tf_op jit(solution)/shard_map/all_gather | solution.py:9
  145.4 6.3 %convolution_convert_fusion = bf16[1024,2048]{1,0:T(8,128)(2,1)} fusion(bf16[1024,512]{0,1:T(8,128)(2,1)} %all-gather.3.cloned.1.call-done, bf16[512,2048]{1,0:T(8,128)(2,1)} %all-gather.5.cloned.1.call-done), kind=kOutput, calls=%fused_computation | convolution fusion | flops 2149580800 | bytes 7340032 | tf_op jit(solution)/shard_map/dot_general | solution.py:10
Async XLA Ops:
  6.5 69.8 %all-gather.3.cloned.1.call-start = ((), (), s32[]{:S(2)}) async-start(), calls=%async_computation | async-start | bytes 1114112 | tf_op jit(solution)/shard_map/all_gather | solution.py:8
  7.3 138.2 %all-gather.5.cloned.1.call-start = ((), (), s32[]{:S(2)}) async-start(), calls=%async_computation.1 | async-start | bytes 2162688 | tf_op jit(solution)/shard_map/all_gather | solution.py:9
Sparse Core Ops, SparseCore 0:
  9.4 66.8 all-gather.2
  79.5 65.8 all-gather.4
where the time goes:
time: 159 us
  waiting for transfers between devices  139 us (87%)
  between operations  13.4 us (8%)
  matrix products  6.32 us (4%)
    all_gather x1, waiting for transfers between devices, on_device(): all_rows = lax.all_gather(rotation, 'grid', axis=0, tiled=True)  69.1 us
    all_gather x1, waiting for transfers between devices, on_device(): all_cols = lax.all_gather(orbitals, 'band', axis=1, tiled=True)  68.3 us
    dot_general x1, matrix products, on_device(): total = jnp.dot(all_cols, all_rows, preferred_element_type=jnp.float32)  6.32 us
  transfers between devices with their start and end apart: 2, of which 2 were waited for; matrix products, arithmetic and copies ran while one was open for 0% of the time, Pallas kernels for 0%

commit v1 on v0

--- a/solution.py
+++ b/solution.py
@@ -6,7 +6,11 @@
 
 def on_device(orbitals, rotation):
     all_cols = lax.all_gather(orbitals, "band", axis=1, tiled=True)
-    all_rows = lax.all_gather(rotation, "grid", axis=0, tiled=True)
+    size = lax.axis_size("grid")
+    repeats = [size if d == 0 else 1 for d in range(rotation.ndim)]
+    all_rows = lax.all_to_all(
+        jnp.tile(rotation, repeats), "grid", split_axis=0, concat_axis=0, tiled=True
+    )
     total = jnp.dot(all_cols, all_rows, preferred_element_type=jnp.float32)
     return total.astype(jnp.bfloat16)
 

time: 159 us -> 108 us (0.68)
  the two profiles are of different devices: /device:TPU:1 before, /device:TPU:2 now
where the time goes in v1:
time: 108 us; the launch traced here: 107 us
  waiting for transfers between devices  76.2 us (71%)
  between operations  13.4 us (12%)
  starting transfers between devices  9.66 us (9%)
  matrix products  5.62 us (5%)
  local copies, waits for them, and re-layouts  2.41 us (2%)
    all_gather x1, waiting for transfers between devices, on_device(): all_cols = lax.all_gather(orbitals, 'band', axis=1, tiled=True)  75.5 us
    all_to_all x1, starting transfers between devices, on_device(): lax.all_to_all(jnp.tile(rotation, repeats), 'grid', split_axis=0, concat_...  9.62 us
    dot_general x1, matrix products, on_device(): total = jnp.dot(all_cols, all_rows, preferred_element_type=jnp.float32)  5.62 us
    another operation x1, local copies, waits for them, and re-layouts, on_device(): jnp.tile(rotation, repeats)  2.41 us
  transfers between devices with their start and end apart: 2, of which 1 were waited for; matrix products, arithmetic and copies ran while one was open for 0% of the time, Pallas kernels for 0%

profile of v1, /device:TPU:2, one launch (start us, length us, event | category | flops | bytes accessed | tf_op | source)
XLA Modules:
  0.0 107.3 jit_solution(8150759165919480075)
XLA Ops:
  6.5 2.4 %tile.2 = bf16[32,16,2048]{2,1,0:T(8,128)(2,1)} broadcast(bf16[16,2048]{1,0:T(8,128)(2,1)} %param.3), dimensions={1,2} | broadcast | bytes 2162688 | tf_op jit(solution)/shard_map/tile | solution.py:12
  8.9 9.6 %all-to-all-start = ((bf16[32,16,2048]{2,1,0:T(8,128)(2,1)}), bf16[32,16,2048]{2,1,0:T(8,128)(2,1)S(1)}, u32[]{:S(2)}, u32[]{:S(2)}) async-start(bf16[32,16,2048]{2,1,0:T(8,128)(2,1)} %tile.2), calls=%async_computation | async-start | bytes 4194304 | tf_op jit(solution)/shard_map/all_to_all | solution.py:11
  18.6 0.0 all-gather.2.cloned.1.call-start
  18.6 0.7 all-gather.2.cloned.1.call-update
  19.3 75.5 %all-gather.2.cloned.1.call-done = bf16[1024,512]{0,1:T(8,128)(2,1)} async-done(((bf16[1024,32]{0,1:T(8,128)(2,1)}), bf16[1024,512]{0,1:T(8,128)(2,1)}) %all-gather.2.cloned.1.call-update) | async-done | bytes 1048592 | tf_op jit(solution)/shard_map/all_gather | solution.py:8
  94.8 0.0 all-to-all-done
  94.8 5.6 %convolution_convert_fusion = bf16[1024,2048]{1,0:T(8,128)(2,1)} fusion(bf16[1024,512]{0,1:T(8,128)(2,1)} %all-gather.2.cloned.1.call-done, bf16[512,2048]{1,0:T(8,128)(2,1)S(1)} %bitcast.3), kind=kOutput, calls=%fused_computation | convolution fusion | flops 2149580800 | bytes 7340032 | tf_op jit(solution)/shard_map/dot_general | solution.py:14
Async XLA Ops:
  8.9 85.9 %all-to-all-start = ((bf16[32,16,2048]{2,1,0:T(8,128)(2,1)}), bf16[32,16,2048]{2,1,0:T(8,128)(2,1)S(1)}, u32[]{:S(2)}, u32[]{:S(2)}) async-start(bf16[32,16,2048]{2,1,0:T(8,128)(2,1)} %tile.2), calls=%async_computation | async-start | bytes 4194304 | tf_op jit(solution)/shard_map/all_to_all | solution.py:11
  18.6 76.2 %all-gather.2.cloned.1.call-start = ((), (), s32[]{:S(2)}) async-start(), calls=%async_computation.1 | async-start | bytes 1114112 | tf_op jit(solution)/shard_map/all_gather | solution.py:8
Sparse Core Ops, SparseCore 0:
  21.5 73.2 all-gather.1
